TPU v7x, 32 devices: a whole 2x2x4 slice. The times are simulated.
32 devices in a mesh: row: 8 (over z, y), col: 4 (over x, core).
Axes of the slice: x: 2, y: 2, z: 4, core: 2. Of those that a mesh axis runs over, the one named last changes fastest.
Arguments:
- ancestor: float32 [1024, 1024], P('row', 'col'), may hold values from -0.1875 to 0.1875
- factor: float32 [1024, 16, 128], P(('row', 'col')), may hold values from -1.5 to 1.5
- diag_inv: float32 [16, 128, 128], replicated, may hold values from -6 to 6
- structure: int32 [16, 96], replicated, may hold values from 0 to 127, as said below
Outputs:
- inverse_panel: float32 [1024, 16, 128], P(('row', 'col'))
- inverse_diagonal: float32 [16, 128, 128], replicated
Inputs may be any that keep to these rules, and one draw needn't show every extreme that they name: Each row of structure lists 96 different block numbers, in no particular order.
All inputs are finite; a program needn't handle non-finite values.
Results may differ from a plain program's by a relative error of at most 0.00007.
Values sent between devices are 32-bit elements; how exact they have to be, the bound alone decides.
A program may use at most 64 MiB of HBM per device.

v0:
```python
import jax
import jax.numpy as jnp
from jax import lax
from jax.sharding import PartitionSpec as P

RB = 8


def per_device(ancestor, factor, diag_inv, structure):
    row_devices = lax.axis_size("row")
    col_devices = lax.axis_size("col")
    ratio = row_devices // col_devices
    local_rows = factor.shape[0]
    width = factor.shape[2]
    first_row = (lax.axis_index("row") * col_devices + lax.axis_index("col")) * local_rows
    block_ids = (first_row + jnp.arange(local_rows, dtype=jnp.int32)) // RB
    matches = block_ids[:, None, None] == structure[None, :, :]
    row_mask = jnp.any(matches, axis=2).astype(jnp.float32)
    masked = factor * row_mask[:, :, None]
    count_sib = masked.shape[1]
    spread = masked.reshape(local_rows, count_sib * width)
    strided = lax.all_gather(spread, "row", axis=0, tiled=True)
    grouped = strided.reshape(col_devices, ratio, local_rows, count_sib * width)
    swapped = lax.all_to_all(grouped, "col", split_axis=0, concat_axis=0, tiled=True)
    columns = jnp.transpose(swapped, (1, 0, 2, 3)).reshape(
        ratio * col_devices * local_rows, count_sib * width
    )
    summed = lax.psum_scatter(
        jnp.dot(
            ancestor, columns, precision=lax.Precision.HIGHEST, preferred_element_type=jnp.float32
        ),
        "col",
        scatter_dimension=0,
        tiled=True,
    )
    panel = -summed.reshape(local_rows, count_sib, width)
    panel = panel * row_mask[:, :, None]
    local_update = jnp.einsum("bsw,bsv->swv", masked, panel, precision=lax.Precision.HIGHEST)
    total_update = lax.psum(local_update, ("row", "col"))
    return (panel, diag_inv - total_update)


def solution(mesh):
    placed = (P("row", "col"), P(("row", "col"), None, None), P(), P())
    return jax.shard_map(
        per_device,
        mesh=mesh,
        in_specs=placed,
        out_specs=(P(("row", "col"), None, None), P()),
        check_vma=False,
    )
```

profile of v0, /device:TPU:0, one launch (start us, length us, event | category | flops | bytes accessed | tf_op | source)
XLA Modules:
  0.0 264.8 jit_solution(8581905215952985030)
XLA Ops:
  7.2 0.0 copy-start
  7.2 0.0 all-gather.2.cloned.1.call-start
  7.2 1.4 compare_reduce_fusion
  8.7 1.1 broadcast_multiply_fusion.1
  9.7 0.8 copy.32
  10.5 0.0 all-gather.2.cloned.1.call-update
  10.6 0.0 reduce-scatter.4.cloned.1.call-start
  10.6 51.9 %all-gather.2.cloned.1.call-done = f32[256,2048]{1,0:T(8,128)} async-done(((f32[32,2048]{1,0:T(8,128)}), f32[256,2048]{1,0:T(8,128)}) %all-gather.2.cloned.1.call-update) | async-done | bytes 2097168 | tf_op jit(solution)/shard_map/all_gather | solution.py:22
  62.5 29.2 %all_to_all.5 = f32[4,2,32,2048]{3,2,1,0:T(8,128)S(1)} all-to-all(f32[4,2,32,2048]{3,2,1,0:T(8,128)} %bitcast.17), channel_id=1, replica_groups=mesh['row'=8,'col'=4] {'col'}, dimensions={0} | all-to-all | bytes 4194304 | tf_op jit(solution)/shard_map/all_to_all | solution.py:24
  91.8 0.2 copy.20
  92.0 0.0 copy-done
  92.0 3.6 %convolution_bitcast_fusion = f32[128,2048]{0,1:T(8,128)S(1)} fusion(f32[256,2048]{1,0:T(8,128)S(1)} %bitcast.14, f32[128,256]{1,0:T(8,128)S(1)} %copy-done), kind=kOutput, calls=%fused_computation | convolution fusion | flops 805306368 | bytes 3276800 | tf_op jit(solution)/shard_map/dot_general | solution.py:29
  95.6 1.3 copy.24
  96.9 0.0 reduce-scatter.4.cloned.1.call-update
  96.9 0.0 all-reduce.2.cloned.1.call-start
  97.0 22.5 %reduce-scatter.4.cloned.1.call-done = f32[32,2048]{1,0:T(8,128)} async-done(((f32[128,2048]{1,0:T(8,128)}), f32[32,2048]{1,0:T(8,128)}) %reduce-scatter.4.cloned.1.call-update) | async-done | bytes 262160
  119.5 1.3 copy.25
  120.8 0.1 neg.6
  120.9 0.0 copy-start.1
  120.9 0.3 copy.21
  121.2 0.1 broadcast_multiply_fusion
  121.3 0.0 copy-start.2
  121.4 2.8 %fusion = f32[16,128,128]{2,1,0:T(8,128)} fusion(f32[32,16,128]{2,1,0:T(8,128)S(1)} %broadcast_multiply_fusion, f32[32,16,128]{2,1,0:T(8,128)S(1)} %broadcast_multiply_fusion.1), kind=kOutput, calls=%fused_computation.2 | convolution fusion | flops 100663296 | bytes 1572864 | tf_op jit(solution)/shard_map/bsw,bsv->swv/dot_general | solution.py:38
  124.1 0.0 all-reduce.2.cloned.1.call-update
  124.2 131.8 %all-reduce.2.cloned.1.call-done = f32[16,128,128]{2,1,0:T(8,128)} async-done(((f32[16,128,128]{2,1,0:T(8,128)}), f32[16,128,128]{2,1,0:T(8,128)}) %all-reduce.2.cloned.1.call-update) | async-done | bytes 1048592 | tf_op jit(solution)/shard_map/psum | solution.py:39
  256.0 0.0 copy-done.1
  256.0 2.3 sub.10
  258.3 0.0 copy-done.2
  (2 shorter events, 0.0 us)
Async XLA Ops:
  7.2 84.8 %copy-start = (f32[128,256]{1,0:T(8,128)S(1)}, f32[128,256]{1,0:T(8,128)}, u32[]{:S(2)}) copy-start(f32[128,256]{1,0:T(8,128)} %param.4) | copy-start | bytes 393220
  7.2 55.3 %all-gather.2.cloned.1.call-start = ((), (), s32[]{:S(2)}) async-start(), calls=%async_computation.2 | async-start | bytes 2359296 | tf_op jit(solution)/shard_map/all_gather | solution.py:22
  10.6 108.9 %reduce-scatter.4.cloned.1.call-start = ((), (), s32[]{:S(2)}) async-start(), calls=%async_computation.4 | async-start | bytes 1310720
  96.9 159.1 %all-reduce.2.cloned.1.call-start = ((), (), s32[]{:S(2)}) async-start(), calls=%async_computation.3 | async-start | bytes 2097152 | tf_op jit(solution)/shard_map/psum | solution.py:39
  120.9 135.1 %copy-start.1 = (f32[16,128,128]{2,1,0:T(8,128)S(1)}, f32[16,128,128]{2,1,0:T(8,128)}, u32[]{:S(2)}) copy-start(f32[16,128,128]{2,1,0:T(8,128)} %param.6) | copy-start | bytes 3145732
  121.3 137.0 %copy-start.2 = (f32[32,16,128]{2,1,0:T(8,128)}, f32[32,16,128]{2,1,0:T(8,128)S(1)}, u32[]{:S(2)}) copy-start(f32[32,16,128]{2,1,0:T(8,128)S(1)} %broadcast_multiply_fusion) | copy-start | bytes 786436
Sparse Core Ops, SparseCore 0:
  10.7 51.7 all-gather.1
  97.1 22.3 reduce-scatter.3
  125.3 130.6 all-reduce.1
where the time goes:
time: 265 us
  waiting for transfers between devices  206 us (78%)
  blocking collectives  29.2 us (11%)
  between operations  13.9 us (5%)
  matrix products  6.38 us (2%)
  other arithmetic  4.99 us (2%)
  local copies, waits for them, and re-layouts  3.94 us (1%)
    psum x1, waiting for transfers between devices, per_device(): total_update = lax.psum(local_update, ('row', 'col'))  132 us
    all_gather x1, waiting for transfers between devices, per_device(): strided = lax.all_gather(spread, 'row', axis=0, tiled=True)  51.9 us
    all_to_all x1, blocking collectives, per_device(): lax.all_to_all(grouped, 'col', split_axis=0, concat_axis=0, tiled=True)  29.2 us
    unnamed x4, waiting for transfers between devices  22.6 us
  transfers between devices with their start and end apart: 3, of which 3 were waited for; matrix products, arithmetic and copies ran while one was open for 0% of the time, Pallas kernels for 0%

commit v1 on v0

--- a/solution.py
+++ b/solution.py
@@ -1,9 +1,17 @@
+import functools
 import jax
 import jax.numpy as jnp
 from jax import lax
 from jax.sharding import PartitionSpec as P
 
 RB = 8
+
+
+def end_the_lots_all(u, device_axis):
+    return jax.lax.all_gather(u, device_axis).sum(axis=0)
+
+
+map_frame = functools.partial(end_the_lots_all, device_axis=("row", "col"))
 
 
 def per_device(ancestor, factor, diag_inv, structure):
@@ -36,7 +44,7 @@
     panel = -summed.reshape(local_rows, count_sib, width)
     panel = panel * row_mask[:, :, None]
     local_update = jnp.einsum("bsw,bsv->swv", masked, panel, precision=lax.Precision.HIGHEST)
-    total_update = lax.psum(local_update, ("row", "col"))
+    total_update = map_frame(local_update)
     return (panel, diag_inv - total_update)
 
 

time: 265 us -> 338 us (1.28)
  waiting for transfers between devices: 206 us -> 269 us
  other arithmetic: 4.99 us -> 15.5 us
    all_gather x0 -> x1, waiting for transfers between devices: none -> 194 us  [end_the_lots_all(): return jax.lax.all_gather(u, device_axis).sum(axis=0)]
    psum x1 -> x0, waiting for transfers between devices: 132 us -> none  [per_device(): total_update = lax.psum(local_update, ('row', 'col'))]
    reduce_sum x0 -> x1, other arithmetic: none -> 11.7 us  [end_the_lots_all(): return jax.lax.all_gather(u, device_axis).sum(axis=0)]
where the time goes in v1:
time: 338 us
  waiting for transfers between devices  269 us (80%)
  blocking collectives  29.2 us (9%)
  other arithmetic  15.5 us (5%)
  between operations  13.9 us (4%)
  matrix products  6.38 us (2%)
  local copies, waits for them, and re-layouts  3.94 us (1%)
    all_gather x1, waiting for transfers between devices, end_the_lots_all(): return jax.lax.all_gather(u, device_axis).sum(axis=0)  194 us
    all_gather x1, waiting for transfers between devices, per_device(): strided = lax.all_gather(spread, 'row', axis=0, tiled=True)  51.9 us
    all_to_all x1, blocking collectives, per_device(): lax.all_to_all(grouped, 'col', split_axis=0, concat_axis=0, tiled=True)  29.2 us
    unnamed x4, waiting for transfers between devices  22.6 us
    reduce_sum x1, other arithmetic, end_the_lots_all(): return jax.lax.all_gather(u, device_axis).sum(axis=0)  11.7 us
  transfers between devices with their start and end apart: 3, of which 3 were waited for; matrix products, arithmetic and copies ran while one was open for 0% of the time, Pallas kernels for 0%

profile of v1, /device:TPU:0, one launch (start us, length us, event | category | flops | bytes accessed | tf_op | source)
XLA Modules:
  0.0 337.8 jit_solution(2080068341328242271)
XLA Ops:
  7.2 0.0 copy-start
  7.2 0.0 all-gather.4.cloned.1.call-start
  7.2 1.4 compare_reduce_fusion
  8.7 1.1 broadcast_multiply_fusion.1
  9.7 0.8 copy.32
  10.5 0.0 all-gather.4.cloned.1.call-update
  10.6 0.0 reduce-scatter.4.cloned.1.call-start
  10.6 51.9 %all-gather.4.cloned.1.call-done = f32[256,2048]{1,0:T(8,128)} async-done(((f32[32,2048]{1,0:T(8,128)}), f32[256,2048]{1,0:T(8,128)}) %all-gather.4.cloned.1.call-update) | async-done | bytes 2097168 | tf_op jit(solution)/shard_map/all_gather | solution.py:30
  62.5 29.2 %all_to_all.5 = f32[4,2,32,2048]{3,2,1,0:T(8,128)S(1)} all-to-all(f32[4,2,32,2048]{3,2,1,0:T(8,128)} %bitcast.19), channel_id=1, replica_groups=mesh['row'=8,'col'=4] {'col'}, dimensions={0} | all-to-all | bytes 4194304 | tf_op jit(solution)/shard_map/all_to_all | solution.py:32
  91.8 0.2 copy.20
  92.0 0.0 copy-done
  92.0 3.6 %convolution_bitcast_fusion = f32[128,2048]{0,1:T(8,128)S(1)} fusion(f32[256,2048]{1,0:T(8,128)S(1)} %bitcast.16, f32[128,256]{1,0:T(8,128)S(1)} %copy-done), kind=kOutput, calls=%fused_computation | convolution fusion | flops 805306368 | bytes 3276800 | tf_op jit(solution)/shard_map/dot_general | solution.py:37
  95.6 1.3 copy.24
  96.9 0.0 reduce-scatter.4.cloned.1.call-update
  96.9 0.0 all-gather.6.cloned.1.call-start
  97.0 22.5 %reduce-scatter.4.cloned.1.call-done = f32[32,2048]{1,0:T(8,128)} async-done(((f32[128,2048]{1,0:T(8,128)}), f32[32,2048]{1,0:T(8,128)}) %reduce-scatter.4.cloned.1.call-update) | async-done | bytes 262160
  119.5 1.3 copy.25
  120.8 0.1 neg.6
  120.9 0.3 copy.21
  121.2 0.1 broadcast_multiply_fusion
  121.3 0.0 copy-start.2
  121.3 2.8 fusion
  124.1 0.0 all-gather.6.cloned.1.call-update
  124.2 194.3 %all-gather.6.cloned.1.call-done = f32[512,128,128]{2,1,0:T(8,128)} async-done(((f32[16,128,128]{2,1,0:T(8,128)}), f32[512,128,128]{2,1,0:T(8,128)}) %all-gather.6.cloned.1.call-update) | async-done | bytes 33554448 | tf_op jit(solution)/shard_map/all_gather | solution.py:11
  318.5 0.0 copy-start.1
  318.5 11.7 %reduce_sum.9 = f32[16,128,128]{2,1,0:T(8,128)S(1)} reduce(f32[32,16,128,128]{3,2,1,0:T(8,128)} %bitcast.14, f32[]{:T(128)} %constant.32.clone.1), dimensions={0}, to_apply=%region_2.3 | reduce | flops 8126464 | bytes 34603012 | tf_op jit(solution)/shard_map/reduce_sum | solution.py:11
  330.2 0.0 copy-done.2
  330.2 0.0 copy-done.1
  330.2 1.1 sub.10
  (2 shorter events, 0.0 us)
Async XLA Ops:
  7.2 84.8 %copy-start = (f32[128,256]{1,0:T(8,128)S(1)}, f32[128,256]{1,0:T(8,128)}, u32[]{:S(2)}) copy-start(f32[128,256]{1,0:T(8,128)} %param.4) | copy-start | bytes 393220
  7.2 55.3 %all-gather.4.cloned.1.call-start = ((), (), s32[]{:S(2)}) async-start(), calls=%async_computation.2 | async-start | bytes 2359296 | tf_op jit(solution)/shard_map/all_gather | solution.py:30
  10.6 108.9 %reduce-scatter.4.cloned.1.call-start = ((), (), s32[]{:S(2)}) async-start(), calls=%async_computation.4 | async-start | bytes 1310720
  96.9 221.5 %all-gather.6.cloned.1.call-start = ((), (), s32[]{:S(2)}) async-start(), calls=%async_computation.3 | async-start | bytes 34603008 | tf_op jit(solution)/shard_map/all_gather | solution.py:11
  121.3 208.9 %copy-start.2 = (f32[32,16,128]{2,1,0:T(8,128)}, f32[32,16,128]{2,1,0:T(8,128)S(1)}, u32[]{:S(2)}) copy-start(f32[32,16,128]{2,1,0:T(8,128)S(1)} %broadcast_multiply_fusion) | copy-start | bytes 786436
  318.5 11.8 %copy-start.1 = (f32[16,128,128]{2,1,0:T(8,128)S(1)}, f32[16,128,128]{2,1,0:T(8,128)}, u32[]{:S(2)}) copy-start(f32[16,128,128]{2,1,0:T(8,128)} %param.6) | copy-start | bytes 3145732
Sparse Core Ops, SparseCore 0:
  10.7 51.7 all-gather.3
  97.1 22.3 reduce-scatter.3
  124.3 194.1 all-gather.5
